TPU v7x, 512 devices: a whole 4x8x8 slice. The times are simulated.
512 devices in a mesh: dp: 8 (over y), row: 4 (over z_lo), col: 16 (over x, z_hi, core).
Axes of the slice: x: 4, y: 8, z: 8 (z_hi: 2, z_lo: 4; z = z_hi * 4 + z_lo), core: 2. Of those that a mesh axis runs over, the one named last changes fastest.
Arguments:
- tokens: bfloat16 [2048, 4096], P(('dp', 'col'), 'row'), may hold values from -6 to 6
- gate_weight: bfloat16 [4096, 14336], P('row', 'col'), may hold values from -0.125 to 0.125
- up_weight: bfloat16 [4096, 14336], P('row', 'col'), may hold values from -0.125 to 0.125
- gate_mask: int32 [32, 112], P('row', 'col'), may hold values 0 or 1
- up_mask: int32 [32, 112], P('row', 'col'), may hold values 0 or 1
- slope: bfloat16 [2048, 14336], P(('dp', 'row'), 'col'), may hold values from -6 to 6
Outputs:
- hidden: bfloat16 [2048, 14336], P(('dp', 'row'), 'col')
- input_grad: bfloat16 [2048, 4096], P(('dp', 'col'), 'row')
- gate_grad: bfloat16 [32, 128, 14336], P('row', 'dp', 'col')
- up_grad: bfloat16 [32, 128, 14336], P('row', 'dp', 'col')
Inputs may be any that keep to these rules, and one draw needn't show every extreme that they name: `gate_mask`: 1 marks a live 128 x 128 block of the projection, 0 a pruned one. `up_mask`: 1 marks a live 128 x 128 block of the projection, 0 a pruned one.
All inputs are finite; a program needn't handle non-finite values.
Results may differ from a plain program's by a relative error of at most 0.0058.
Values may be sent and summed in bfloat16 or wider, within the bound.
No kernel may reach another device: no remote copies, remote signals or barrier semaphores. Data moves between devices by JAX's collectives and lax.ppermute only.
A program may use at most 64 MiB of HBM per device.

v0:
```python
import jax
import jax.numpy as jnp
from jax import lax
from jax.sharding import PartitionSpec as P


def expand_mask(mask, block, height):
    blocks_down, blocks_across = mask.shape
    grid = mask.astype(jnp.float32)[:, None, :, None]
    return jnp.broadcast_to(grid, (blocks_down, height, blocks_across, block)).reshape(
        blocks_down, height, blocks_across * block
    )


def body(tokens, gate_weight, up_weight, gate_mask, up_mask, slope):
    block = gate_weight.shape[0] // gate_mask.shape[0]
    width_part = gate_weight.shape[0]
    hidden_part = gate_weight.shape[1]
    gate_live = (
        gate_weight.astype(jnp.float32)
        * expand_mask(gate_mask, block, block).reshape(width_part, hidden_part)
    ).astype(jnp.bfloat16)
    up_live = (
        up_weight.astype(jnp.float32)
        * expand_mask(up_mask, block, block).reshape(width_part, hidden_part)
    ).astype(jnp.bfloat16)
    paired = jnp.concatenate([gate_live, up_live], axis=1)
    gathered = lax.all_gather(tokens, "col", axis=0, tiled=True)
    replica_tokens = gathered.shape[0]
    rows_here = gathered
    sums = lax.psum_scatter(
        jnp.dot(rows_here, paired, preferred_element_type=jnp.float32),
        "row",
        scatter_dimension=0,
        tiled=True,
    )
    gate = sums[:, :hidden_part]
    up = sums[:, hidden_part:]
    sigma = jax.nn.sigmoid(gate)
    act = gate * sigma
    hidden = (act * up).astype(jnp.bfloat16)
    slope_wide = slope.astype(jnp.float32)
    gate_slope = (slope_wide * up * sigma * (1.0 + gate * (1.0 - sigma))).astype(jnp.bfloat16)
    up_slope = (slope_wide * act).astype(jnp.bfloat16)
    slopes = jnp.concatenate([gate_slope, up_slope], axis=1)
    replica = lax.axis_index("dp")
    replicas = lax.axis_size("dp")
    share = block // replicas
    blocks_down = width_part // block
    everyone = lax.all_gather(slopes, ("dp", "row"), axis=0, tiled=True)
    local_slopes = lax.dynamic_slice_in_dim(everyone, replica * replica_tokens, replica_tokens, 0)
    by_owner = gathered.reshape(replica_tokens, blocks_down, replicas, share)
    by_owner = jnp.transpose(by_owner, (2, 0, 1, 3)).reshape(
        replicas, replica_tokens, blocks_down * share
    )
    feats = lax.all_to_all(by_owner, "dp", split_axis=0, concat_axis=0, tiled=True)
    partial_value = jnp.einsum(
        "ptk,ptf->pkf",
        feats,
        everyone.reshape(replicas, replica_tokens, -1),
        preferred_element_type=jnp.float32,
    )
    rounded = lax.optimization_barrier(partial_value.astype(jnp.bfloat16))
    grads = jnp.sum(rounded.astype(jnp.float32), axis=0).reshape(
        blocks_down, share, 2 * hidden_part
    )
    rows_here = local_slopes
    input_grad = lax.psum_scatter(
        lax.dot_general(
            rows_here, paired, (((1,), (1,)), ((), ())), preferred_element_type=jnp.float32
        ),
        "col",
        scatter_dimension=0,
        tiled=True,
    ).astype(jnp.bfloat16)
    gate_grad = (grads[:, :, :hidden_part] * expand_mask(gate_mask, block, share)).astype(
        jnp.bfloat16
    )
    up_grad = (grads[:, :, hidden_part:] * expand_mask(up_mask, block, share)).astype(jnp.bfloat16)
    return (hidden, input_grad, gate_grad, up_grad)


def solution(mesh):
    return jax.shard_map(
        body,
        mesh=mesh,
        in_specs=(
            P(("dp", "col"), "row"),
            P("row", "col"),
            P("row", "col"),
            P("row", "col"),
            P("row", "col"),
            P(("dp", "row"), "col"),
        ),
        out_specs=(
            P(("dp", "row"), "col"),
            P(("dp", "col"), "row"),
            P("row", "dp", "col"),
            P("row", "dp", "col"),
        ),
        check_vma=False,
    )
```

profile of v0, /device:TPU:8, one launch (start us, length us, event | category | flops | bytes accessed | tf_op | source)
XLA Modules:
  0.0 386.7 jit_solution(408374661671901712)
XLA Ops:
  7.2 39.3 %all_gather.6 = bf16[256,1024]{1,0:T(8,128)(2,1)S(1)} all-gather(bf16[16,1024]{1,0:T(8,128)(2,1)} %param.6), channel_id=1, replica_groups=mesh['dp'=8,'row'=4,'col'=16] {'col'}, dimensions={0}, use_global_device_ids=true | all-gather | bytes 557056 | tf_op jit(solution)/shard_map/all_gather | solution.py:28
  46.5 0.7 convert_element_type.54
  47.3 2.9 copy.44
  50.3 3.8 copy.42
  54.1 0.3 broadcast_in_dim.33
  54.4 0.3 broadcast_in_dim.32
  54.7 0.9 copy-done
  55.6 2.5 fusion
  58.1 1.2 copy-done.1
  59.3 0.6 copy-done.3
  59.9 1.2 convolution_bitcast_fusion
  61.1 1.7 copy.57
  63.0 0.8 copy.46
  63.8 43.9 %reduce-scatter.7.cloned.1.call-done = f32[64,1792]{1,0:T(8,128)} async-done(((f32[256,1792]{1,0:T(8,128)}), f32[64,1792]{1,0:T(8,128)}) %reduce-scatter.7.cloned.1.call-update) | async-done | bytes 458768
  107.7 1.1 fusion.15
  108.8 0.2 copy.60
  109.0 0.2 copy.59
  109.2 1.4 fusion.7
  110.6 0.1 pad_maximum_fusion.3
  110.7 0.9 copy.47
  111.6 0.2 copy.48
  111.8 1.0 copy.50
  112.8 7.3 %all-to-all-start = ((bf16[8,256,128]{2,1,0:T(8,128)(2,1)}), bf16[8,256,128]{2,1,0:T(8,128)(2,1)S(1)}, u32[]{:S(2)}, u32[]{:S(2)}) async-start(bf16[8,256,128]{2,1,0:T(8,128)(2,1)} %copy.50), calls=%async_computation.1 | async-start | bytes 1048576 | tf_op jit(solution)/shard_map/all_to_all | solution.py:56
  120.1 165.6 %all-gather.2.cloned.1.call-done = bf16[2048,1792]{1,0:T(8,128)(2,1)} async-done(((bf16[64,1792]{1,0:T(8,128)(2,1)}), bf16[2048,1792]{1,0:T(8,128)(2,1)}) %all-gather.2.cloned.1.call-update) | async-done | bytes 7340048 | tf_op jit(solution)/shard_map/all_gather | solution.py:50
  285.7 3.9 %fusion.3 = f32[256,1024]{1,0:T(8,128)} fusion(bf16[1024,896]{0,1:T(8,128)(2,1)S(1)} %copy-done.2, bf16[1024,896]{0,1:T(8,128)(2,1)} %copy-done.3, bf16[2048,1792]{1,0:T(8,128)(2,1)} %all-gather.2.cloned.1.call-done, s32[]{:T(128)S(6)} %select_n.3), kind=kOutput, calls=%fused_computation.9 | convolution fusion | flops 946864128 | bytes 5636100 | tf_op jit(solution)/shard_map/dot_general | solution.py:69
  289.7 0.8 copy.55
  290.5 5.5 %fusion.2 = bf16[8,128,1792]{1,2,0:T(8,128)(2,1)S(1)} fusion(bf16[8,256,1792]{2,1,0:T(8,128)(2,1)} %bitcast.36, bf16[8,256,128]{2,1,0:T(8,128)(2,1)S(1)} %all-to-all-done), kind=kOutput, calls=%fused_computation.7 | convolution fusion | flops 941359104 | bytes 11534336 | tf_op jit(solution)/shard_map/ptk,ptf->pkf/dot_general | solution.py:57
  296.0 0.5 convert_reduce_fusion
  296.5 0.3 copy.52
  296.9 0.8 fusion.9
  297.7 81.0 %reduce-scatter.5.cloned.1.call-done = f32[16,1024]{1,0:T(8,128)} async-done(((f32[256,1024]{1,0:T(8,128)}), f32[16,1024]{1,0:T(8,128)}) %reduce-scatter.5.cloned.1.call-update) | async-done | bytes 65552 | tf_op jit(solution)/shard_map/reduce_scatter | solution.py:68
  378.7 1.5 convert_element_type.60
  (21 shorter events, 0.4 us)
Async XLA Ops:
  7.2 43.0 %copy-start.5 = (s32[8,7]{1,0:T(8,128)S(1)}, s32[8,7]{1,0:T(8,128)}, u32[]{:S(2)}) copy-start(s32[8,7]{1,0:T(8,128)} %param.9) | copy-start | bytes 676
  7.2 100.5 %reduce-scatter.7.cloned.1.call-start = ((), (), s32[]{:S(2)}) async-start(), calls=%async_computation.5 | async-start | bytes 2293760
  54.1 1.5 copy-start
  58.1 1.2 copy-start.1
  58.1 1.8 copy-start.3
  61.1 1.8 copy-start.4
  62.9 222.8 %all-gather.2.cloned.1.call-start = ((), (), s32[]{:S(2)}) async-start(), calls=%async_computation.3 | async-start | bytes 7569408 | tf_op jit(solution)/shard_map/all_gather | solution.py:50
  109.2 176.5 %copy-start.2 = (bf16[1024,896]{0,1:T(8,128)(2,1)S(1)}, bf16[1024,896]{0,1:T(8,128)(2,1)}, u32[]{:S(2)}) copy-start(bf16[1024,896]{0,1:T(8,128)(2,1)} %copy-done.1) | copy-start | bytes 5505028
  112.8 177.7 %all-to-all-start = ((bf16[8,256,128]{2,1,0:T(8,128)(2,1)}), bf16[8,256,128]{2,1,0:T(8,128)(2,1)S(1)}, u32[]{:S(2)}, u32[]{:S(2)}) async-start(bf16[8,256,128]{2,1,0:T(8,128)(2,1)} %copy.50), calls=%async_computation.1 | async-start | bytes 1048576 | tf_op jit(solution)/shard_map/all_to_all | solution.py:56
  120.1 258.6 %reduce-scatter.5.cloned.1.call-start = ((), (), s32[]{:S(2)}) async-start(), calls=%async_computation.4 | async-start | bytes 1114112 | tf_op jit(solution)/shard_map/reduce_scatter | solution.py:68
Sparse Core Ops, SparseCore 0:
  63.0 44.6 reduce-scatter.6
  111.7 173.9 all-gather.1
  290.4 88.1 reduce-scatter.4
where the time goes:
time: 387 us
  waiting for transfers between devices  291 us (75%)
  blocking collectives  39.3 us (10%)
  local copies, waits for them, and re-layouts  17.5 us (5%)
  between operations  13.9 us (4%)
  matrix products  10.6 us (3%)
  other arithmetic  7.47 us (2%)
  starting transfers between devices  7.34 us (2%)
    all_gather x1, waiting for transfers between devices, body(): everyone = lax.all_gather(slopes, ('dp', 'row'), axis=0, tiled=True)  166 us
    reduce_scatter x1, waiting for transfers between devices, body(): lax.psum_scatter(lax.dot_general(rows_here, paired, (((1,), (1,)), ((), (...  81 us
    unnamed x4, waiting for transfers between devices  44 us
    all_gather x1, blocking collectives, body(): gathered = lax.all_gather(tokens, 'col', axis=0, tiled=True)  39.3 us
    unnamed x19, local copies, waits for them, and re-layouts  13.2 us
  transfers between devices with their start and end apart: 4, of which 3 were waited for; matrix products, arithmetic and copies ran while one was open for 4% of the time, Pallas kernels for 0%

commit v1 on v0

--- a/solution.py
+++ b/solution.py
@@ -25,7 +25,9 @@
         * expand_mask(up_mask, block, block).reshape(width_part, hidden_part)
     ).astype(jnp.bfloat16)
     paired = jnp.concatenate([gate_live, up_live], axis=1)
-    gathered = lax.all_gather(tokens, "col", axis=0, tiled=True)
+    gathered = jnp.concatenate(
+        lax.all_to_all(jnp.stack([tokens] * lax.axis_size("col")), "col", 0, 0), axis=0
+    )
     replica_tokens = gathered.shape[0]
     rows_here = gathered
     sums = lax.psum_scatter(

time: 387 us -> 372 us (0.961)
  blocking collectives: 39.3 us -> 0 us
  starting transfers between devices: 7.34 us -> 20.2 us
  local copies, waits for them, and re-layouts: 17.5 us -> 26 us
    all_gather x1 -> x0, blocking collectives: 39.3 us -> none  [body(): gathered = lax.all_gather(tokens, 'col', axis=0, tiled=True)]
    all_to_all x0 -> x1, starting transfers between devices: none -> 12.8 us  [body(): lax.all_to_all(jnp.stack([tokens] * lax.axis_size('col')), 'col', 0, 0)]
    all_gather x1, waiting for transfers between devices: 166 us -> 157 us  [body(): everyone = lax.all_gather(slopes, ('dp', 'row'), axis=0, tiled=True)]
    another operation x0 -> x2, local copies, waits for them, and re-layouts: none -> 6.22 us  [the longest x1 4.6 us: body(): by_owner = gathered.reshape(replica_tokens, blocks_down, replicas, share)]
    unnamed x4, waiting for transfers between devices: 44 us -> 49 us
    transpose x1, local copies, waits for them, and re-layouts: 0.04 us -> 4.99 us  [body(): jnp.transpose(by_owner, (2, 0, 1, 3))]
    unnamed x19 -> x15, local copies, waits for them, and re-layouts: 13.2 us -> 10.7 us
  transfers between devices with their start and end apart: 4 -> 5, of which waited for: 3 -> 4; matrix products, arithmetic and copies ran while one was open for 4% -> 9% of each run, Pallas kernels for 0% -> 0%
where the time goes in v1:
time: 372 us; the launch traced here: 371 us
  waiting for transfers between devices  291 us (78%)
  local copies, waits for them, and re-layouts  26 us (7%)
  starting transfers between devices  20.2 us (5%)
  between operations  13.9 us (4%)
  matrix products  12.6 us (3%)
  other arithmetic  7.75 us (2%)
    all_gather x1, waiting for transfers between devices, body(): everyone = lax.all_gather(slopes, ('dp', 'row'), axis=0, tiled=True)  157 us
    reduce_scatter x1, waiting for transfers between devices, body(): lax.psum_scatter(lax.dot_general(rows_here, paired, (((1,), (1,)), ((), (...  82.7 us
    unnamed x4, waiting for transfers between devices  49 us
    all_to_all x1, starting transfers between devices, body(): lax.all_to_all(jnp.stack([tokens] * lax.axis_size('col')), 'col', 0, 0)  12.8 us
    unnamed x15, local copies, waits for them, and re-layouts  10.7 us
  transfers between devices with their start and end apart: 5, of which 4 were waited for; matrix products, arithmetic and copies ran while one was open for 9% of the time, Pallas kernels for 0%

profile of v1, /device:TPU:8, one launch (start us, length us, event | category | flops | bytes accessed | tf_op | source)
XLA Modules:
  0.0 371.1 jit_solution(16951294824687486178)
XLA Ops:
  7.2 1.6 stack.2
  8.8 12.8 %all-to-all-start = ((bf16[16,16,1024]{2,1,0:T(8,128)(2,1)}), bf16[16,16,1024]{2,1,0:T(8,128)(2,1)S(1)}, u32[]{:S(2)}, u32[]{:S(2)}) async-start(bf16[16,16,1024]{2,1,0:T(8,128)(2,1)} %stack.2), calls=%async_computation | async-start | bytes 1048576 | tf_op jit(solution)/shard_map/all_to_all | solution.py:29
  21.7 0.7 convert_element_type.54
  22.5 2.9 copy.41
  25.5 3.8 %copy.39 = bf16[1024,896]{0,1:T(8,128)(2,1)} copy(bf16[1024,896]{1,0:T(8,128)(2,1)} %param.7) | data formatting | bytes 3670016 | tf_op args[1]
  29.3 0.3 broadcast_in_dim.33
  29.6 0.3 broadcast_in_dim.32
  29.9 0.9 copy-done
  30.8 3.8 %fusion = (bf16[1024,896]{0,1:T(8,128)(2,1)}, bf16[1024,896]{0,1:T(8,128)(2,1)}) fusion(f32[112,8,8,128]{3,2,1,0:T(8,128)S(1)} %bitcast.34, bf16[1024,896]{0,1:T(8,128)(2,1)S(1)} %copy.41, f32[112,8,8,128]{3,2,1,0:T(8,128)S(1)} %bitcast.35, bf16[1024,896]{0,1:T(8,128)(2,1)S(1)} %copy-done), kind=kLoop, calls=%fused_computation.3 | loop fusion | flops 5505024 | bytes 14680064 | tf_op jit(solution)/shard_map/convert_element_type | solution.py:26
  34.6 1.9 all-to-all-done
  36.5 3.2 convolution_bitcast_fusion
  39.7 1.7 copy.53
  41.6 0.2 copy.43
  41.7 49.0 %reduce-scatter.7.cloned.1.call-done = f32[64,1792]{1,0:T(8,128)} async-done(((f32[256,1792]{1,0:T(8,128)}), f32[64,1792]{1,0:T(8,128)}) %reduce-scatter.7.cloned.1.call-update) | async-done | bytes 458768
  90.7 1.1 fusion.15
  91.8 0.2 copy.56
  92.0 0.2 copy.55
  92.2 0.3 fusion.7
  92.7 0.9 copy.44
  93.6 4.6 %reshape_reshape.11 = bf16[256,8,8,16]{3,2,1,0:T(8,128)(2,1)} reshape(bf16[16,16,1024]{2,1,0:T(8,128)(2,1)S(1)} %all-to-all-done) | data formatting | bytes 1048576 | tf_op jit(solution)/shard_map/reshape;reshape | solution.py:54
  98.2 5.0 %copy.45 = bf16[8,256,8,16]{1,3,2,0:T(8,128)(2,1)S(1)} copy(bf16[8,256,8,16]{3,0,2,1:T(8,128)(2,1)} %bitcast.33) | data formatting | bytes 1048576 | tf_op jit(solution)/shard_map/transpose | solution.py:55
  103.2 1.0 copy.46
  104.2 7.3 %all-to-all-start.1 = ((bf16[8,256,128]{2,1,0:T(8,128)(2,1)}), bf16[8,256,128]{2,1,0:T(8,128)(2,1)S(1)}, u32[]{:S(2)}, u32[]{:S(2)}) async-start(bf16[8,256,128]{2,1,0:T(8,128)(2,1)} %copy.46), calls=%async_computation.2 | async-start | bytes 1048576 | tf_op jit(solution)/shard_map/all_to_all | solution.py:58
  111.5 157.0 %all-gather.2.cloned.1.call-done = bf16[2048,1792]{1,0:T(8,128)(2,1)} async-done(((bf16[64,1792]{1,0:T(8,128)(2,1)}), bf16[2048,1792]{1,0:T(8,128)(2,1)}) %all-gather.2.cloned.1.call-update) | async-done | bytes 7340048 | tf_op jit(solution)/shard_map/all_gather | solution.py:52
  268.4 3.9 %fusion.3 = f32[256,1024]{1,0:T(8,128)} fusion(bf16[1024,896]{0,1:T(8,128)(2,1)S(1)} %copy-done.1, bf16[1024,896]{0,1:T(8,128)(2,1)} %get-tuple-element.28, bf16[2048,1792]{1,0:T(8,128)(2,1)} %all-gather.2.cloned.1.call-done, s32[]{:T(128)S(6)} %select_n.3), kind=kOutput, calls=%fused_computation.9 | convolution fusion | flops 946864128 | bytes 5636100 | tf_op jit(solution)/shard_map/dot_general | solution.py:71
  272.4 0.8 copy.51
  273.2 5.5 %fusion.2 = bf16[8,128,1792]{1,2,0:T(8,128)(2,1)S(1)} fusion(bf16[8,256,1792]{2,1,0:T(8,128)(2,1)} %bitcast.36, bf16[8,256,128]{2,1,0:T(8,128)(2,1)S(1)} %all-to-all-done.1), kind=kOutput, calls=%fused_computation.7 | convolution fusion | flops 941359104 | bytes 11534336 | tf_op jit(solution)/shard_map/ptk,ptf->pkf/dot_general | solution.py:59
  278.7 0.5 convert_reduce_fusion
  279.3 0.3 copy.48
  279.6 0.8 fusion.9
  280.4 82.7 %reduce-scatter.5.cloned.1.call-done = f32[16,1024]{1,0:T(8,128)} async-done(((f32[256,1024]{1,0:T(8,128)}), f32[16,1024]{1,0:T(8,128)}) %reduce-scatter.5.cloned.1.call-update) | async-done | bytes 65552 | tf_op jit(solution)/shard_map/reduce_scatter | solution.py:70
  363.1 1.5 convert_element_type.60
  (19 shorter events, 0.5 us)
Async XLA Ops:
  7.2 18.2 %copy-start.3 = (s32[8,7]{1,0:T(8,128)S(1)}, s32[8,7]{1,0:T(8,128)}, u32[]{:S(2)}) copy-start(s32[8,7]{1,0:T(8,128)} %param.9) | copy-start | bytes 676
  8.8 27.7 %all-to-all-start = ((bf16[16,16,1024]{2,1,0:T(8,128)(2,1)}), bf16[16,16,1024]{2,1,0:T(8,128)(2,1)S(1)}, u32[]{:S(2)}, u32[]{:S(2)}) async-start(bf16[16,16,1024]{2,1,0:T(8,128)(2,1)} %stack.2), calls=%async_computation | async-start | bytes 1048576 | tf_op jit(solution)/shard_map/all_to_all | solution.py:29
  21.7 69.1 %reduce-scatter.7.cloned.1.call-start = ((), (), s32[]{:S(2)}) async-start(), calls=%async_computation.6 | async-start | bytes 2293760
  29.3 1.5 copy-start
  39.7 1.8 copy-start.2
  41.5 226.9 %all-gather.2.cloned.1.call-start = ((), (), s32[]{:S(2)}) async-start(), calls=%async_computation.4 | async-start | bytes 7569408 | tf_op jit(solution)/shard_map/all_gather | solution.py:52
  98.2 170.3 %copy-start.1 = (bf16[1024,896]{0,1:T(8,128)(2,1)S(1)}, bf16[1024,896]{0,1:T(8,128)(2,1)}, u32[]{:S(2)}) copy-start(bf16[1024,896]{0,1:T(8,128)(2,1)} %get-tuple-element.27) | copy-start | bytes 5505028
  104.2 169.0 %all-to-all-start.1 = ((bf16[8,256,128]{2,1,0:T(8,128)(2,1)}), bf16[8,256,128]{2,1,0:T(8,128)(2,1)S(1)}, u32[]{:S(2)}, u32[]{:S(2)}) async-start(bf16[8,256,128]{2,1,0:T(8,128)(2,1)} %copy.46), calls=%async_computation.2 | async-start | bytes 1048576 | tf_op jit(solution)/shard_map/all_to_all | solution.py:58
  111.5 251.7 %reduce-scatter.5.cloned.1.call-start = ((), (), s32[]{:S(2)}) async-start(), calls=%async_computation.5 | async-start | bytes 1114112 | tf_op jit(solution)/shard_map/reduce_scatter | solution.py:70
Sparse Core Ops, SparseCore 0:
  41.6 49.0 reduce-scatter.6
  93.7 174.6 all-gather.1
  273.1 89.9 reduce-scatter.4
